TPU v7x, 32 devices: a whole 2x2x4 slice. The times are simulated.
32 devices in a mesh: dp: 8 (over z, x), tensor: 4 (over y, core).
Axes of the slice: x: 2, y: 2, z: 4, core: 2. Of those that a mesh axis runs over, the one named last changes fastest.
Arguments:
- hidden_in: bfloat16 [4096, 1024], P(('dp', 'tensor')), may hold values from -8 to 8
- cotangent: bfloat16 [4096, 1024], P(('dp', 'tensor')), may hold values from -6 to 6
- lengths: int32 [8], P('dp'), may hold values from 128 to 512, as said below
- query_weight: bfloat16 [1024, 1024], P('dp', 'tensor'), as said below
- key_weight: bfloat16 [1024, 1024], P('dp', 'tensor'), as said below
- value_weight: bfloat16 [1024, 1024], P('dp', 'tensor'), may hold values from -0.1875 to 0.1875
- output_weight: bfloat16 [1024, 1024], P('tensor', 'dp'), may hold values from -1 to 1
- up_weight: bfloat16 [1024, 4096], P('dp', 'tensor'), may hold values from -0.1875 to 0.1875
- down_weight: bfloat16 [4096, 1024], P('tensor', 'dp'), may hold values from -0.09375 to 0.09375
- query_bias: float32 [1024], P('tensor'), may hold values from -3 to 3
- value_bias: float32 [1024], P('tensor'), may hold values from -3 to 3
- output_bias: float32 [1024], replicated, may hold values from -3 to 3
- up_bias: float32 [4096], P('tensor'), may hold values from -3 to 3
- down_bias: float32 [1024], replicated, may hold values from -3 to 3
- first_gain: float32 [1024], replicated, may hold values from 0.5 to 1.5
- first_shift: float32 [1024], replicated, may hold values from -3 to 3
- second_gain: float32 [1024], replicated, may hold values from 0.5 to 1.5
- second_shift: float32 [1024], replicated, may hold values from -3 to 3
Outputs:
- hidden_out: bfloat16 [4096, 1024], P(('dp', 'tensor'))
- grad_in: bfloat16 [4096, 1024], P(('dp', 'tensor'))
- grad_query_weight: float32 [1024, 1024], P('dp', 'tensor')
- grad_key_weight: float32 [1024, 1024], P('dp', 'tensor')
- grad_value_weight: float32 [1024, 1024], P('dp', 'tensor')
- grad_output_weight: float32 [1024, 1024], P('tensor', 'dp')
- grad_up_weight: float32 [1024, 4096], P('dp', 'tensor')
- grad_down_weight: float32 [4096, 1024], P('tensor', 'dp')
- grad_query_bias: float32 [1024], P('tensor')
- grad_value_bias: float32 [1024], P('tensor')
- grad_output_bias: float32 [1024], replicated
- grad_up_bias: float32 [4096], P('tensor')
- grad_down_bias: float32 [1024], replicated
- grad_first_gain: float32 [1024], replicated
- grad_first_shift: float32 [1024], replicated
- grad_second_gain: float32 [1024], replicated
- grad_second_shift: float32 [1024], replicated
Inputs may be any that keep to these rules, and one draw needn't show every extreme that they name: `lengths`: positions of a sequence at or past its entry are padding keys. Some sequence is full. `query_weight`: A projection scaled by its fan-in. `key_weight`: A projection scaled by its fan-in.
All inputs are finite; a program needn't handle non-finite values.
Results may differ from a plain program's by a relative error of at most 0.02.
Values may be sent and summed in bfloat16 or wider, within the bound.
No kernel may reach another device: no remote copies, remote signals or barrier semaphores. Data moves between devices by JAX's collectives and lax.ppermute only.
A program may use at most 128 MiB of HBM per device.

v0:
```python
import jax
import jax.numpy as jnp
from jax import lax
from jax.sharding import PartitionSpec as P

HD = 64
EPSILON = 1e-12
ROOT_HALF = 0.7071067811865476
INV_ROOT_TWO_PI = 0.3989422804014327
MASKED = -1e30


def matmul(left_side, right_side):
    return jnp.dot(left_side, right_side, preferred_element_type=jnp.float32)


def matmul_nt(left_side, right_side):
    return lax.dot_general(
        left_side, right_side, (((1,), (1,)), ((), ())), preferred_element_type=jnp.float32
    )


def matmul_tn(left_side, right_side):
    return lax.dot_general(
        left_side, right_side, (((0,), (0,)), ((), ())), preferred_element_type=jnp.float32
    )


def gelu_value(pre_act):
    return pre_act * 0.5 * (1.0 + lax.erf(pre_act * ROOT_HALF))


def gelu_slope(pre_act):
    cumulative = 0.5 * (1.0 + lax.erf(pre_act * ROOT_HALF))
    density = jnp.exp(-0.5 * pre_act * pre_act) * INV_ROOT_TWO_PI
    return cumulative + pre_act * density


def norm_forward(summed, gain_vector, shift_vector):
    centre = summed - jnp.mean(summed, axis=-1, keepdims=True)
    spread = jnp.mean(centre * centre, axis=-1, keepdims=True)
    inverse = lax.rsqrt(spread + EPSILON)
    normed = centre * inverse
    return (normed * gain_vector + shift_vector, normed, inverse)


def norm_backward(upstream, gain_vector, normed, inverse):
    scaled = upstream * gain_vector
    return inverse * (
        scaled
        - jnp.mean(scaled, axis=-1, keepdims=True)
        - normed * jnp.mean(scaled * normed, axis=-1, keepdims=True)
    )


def fetch_weights(query_weight, key_weight, value_weight, up_weight, output_weight, down_weight):
    row_parts = (
        lax.all_gather(query_weight, "dp", axis=0, tiled=True),
        lax.all_gather(key_weight, "dp", axis=0, tiled=True),
        lax.all_gather(value_weight, "dp", axis=0, tiled=True),
        lax.all_gather(up_weight, "dp", axis=0, tiled=True),
    )
    col_parts = (
        lax.all_gather(output_weight, "dp", axis=1, tiled=True),
        lax.all_gather(down_weight, "dp", axis=1, tiled=True),
    )
    return (row_parts, col_parts)


def masked_scores(query_block, key_heads, key_valid, score_scale):
    scores = (
        jnp.einsum("qhd,khd->hqk", query_block, key_heads, preferred_element_type=jnp.float32)
        * score_scale
    )
    return jnp.where(key_valid[None, None, :], scores, MASKED)


def widen(vector, tensor_index, n_tensor):
    zeros_full = jnp.zeros((n_tensor * vector.shape[0],), jnp.float32)
    return lax.dynamic_update_slice_in_dim(zeros_full, vector, tensor_index * vector.shape[0], 0)


def shards(
    hidden_in,
    cotangent,
    lengths,
    query_weight,
    key_weight,
    value_weight,
    output_weight,
    up_weight,
    down_weight,
    query_bias,
    value_bias,
    output_bias,
    up_bias,
    down_bias,
    first_gain,
    first_shift,
    second_gain,
    second_shift,
):
    n_tensor = lax.axis_size("tensor")
    tensor_index = lax.axis_index("tensor")
    local_rows = hidden_in.shape[0]
    seq_len = local_rows * n_tensor
    local_width = query_weight.shape[1]
    local_heads = local_width // HD
    score_scale = HD ** (-0.5)
    length = lengths[0]
    key_valid = jnp.arange(seq_len, dtype=jnp.int32) < length
    row_parts, col_parts = fetch_weights(
        query_weight, key_weight, value_weight, up_weight, output_weight, down_weight
    )
    query_full, key_full, value_full, up_full = row_parts
    output_full, down_full = col_parts
    hidden_full = lax.all_gather(hidden_in, "tensor", axis=0, tiled=True)
    queries = (matmul(hidden_full, query_full) + query_bias).astype(jnp.bfloat16)
    key_rows = matmul(hidden_full, key_full).astype(jnp.bfloat16)
    value_rows = (matmul(hidden_full, value_full) + value_bias).astype(jnp.bfloat16)
    query_heads = queries.reshape(seq_len, local_heads, HD)
    key_heads = key_rows.reshape(seq_len, local_heads, HD)
    value_heads = value_rows.reshape(seq_len, local_heads, HD)
    scores = masked_scores(query_heads, key_heads, key_valid, score_scale)
    row_peak = jnp.max(scores, axis=-1, keepdims=True)
    log_total = row_peak + jnp.log(jnp.sum(jnp.exp(scores - row_peak), axis=-1, keepdims=True))
    probs_low = jnp.exp(scores - log_total).astype(jnp.bfloat16)
    context_block = jnp.einsum(
        "hqk,khd->qhd", probs_low, value_heads, preferred_element_type=jnp.float32
    )
    context_parts = context_block.astype(jnp.bfloat16)
    context = context_parts.reshape(seq_len, local_width)
    attn_rows = lax.psum_scatter(
        matmul(context, output_full).astype(jnp.bfloat16), "tensor", scatter_dimension=0, tiled=True
    ).astype(jnp.float32)
    first_sum = hidden_in.astype(jnp.float32) + attn_rows + output_bias
    first_out, first_normed, first_inverse = norm_forward(first_sum, first_gain, first_shift)
    first_low = first_out.astype(jnp.bfloat16)
    normed_full = lax.all_gather(first_low, "tensor", axis=0, tiled=True)
    pre_act = matmul(normed_full, up_full) + up_bias
    activated = gelu_value(pre_act).astype(jnp.bfloat16)
    mlp_rows = lax.psum_scatter(
        matmul(activated, down_full).astype(jnp.bfloat16), "tensor", scatter_dimension=0, tiled=True
    ).astype(jnp.float32)
    second_sum = first_out + mlp_rows + down_bias
    second_out, second_normed, second_inverse = norm_forward(second_sum, second_gain, second_shift)
    hidden_out = second_out.astype(jnp.bfloat16)
    upstream = cotangent.astype(jnp.float32)
    grad_second_gain = jnp.sum(upstream * second_normed, axis=0)
    grad_second_shift = jnp.sum(upstream, axis=0)
    second_grad = norm_backward(upstream, second_gain, second_normed, second_inverse)
    grad_down_bias = jnp.sum(second_grad, axis=0)
    second_low = second_grad.astype(jnp.bfloat16)
    second_full = lax.all_gather(second_low, "tensor", axis=0, tiled=True)
    grad_down = matmul_tn(activated, second_full)
    pre_grad = matmul_nt(second_full, down_full) * gelu_slope(pre_act)
    grad_up_bias = jnp.sum(pre_grad, axis=0)
    pre_low = pre_grad.astype(jnp.bfloat16)
    grad_up = matmul_tn(normed_full, pre_low)
    first_grad_in = second_grad + lax.psum_scatter(
        matmul_nt(pre_low, up_full).astype(jnp.bfloat16), "tensor", scatter_dimension=0, tiled=True
    ).astype(jnp.float32)
    grad_first_gain = jnp.sum(first_grad_in * first_normed, axis=0)
    grad_first_shift = jnp.sum(first_grad_in, axis=0)
    first_grad = norm_backward(first_grad_in, first_gain, first_normed, first_inverse)
    grad_output_bias = jnp.sum(first_grad, axis=0)
    first_grad_low = first_grad.astype(jnp.bfloat16)
    attn_grad_full = lax.all_gather(first_grad_low, "tensor", axis=0, tiled=True)
    grad_output = matmul_tn(context, attn_grad_full)
    context_grad = matmul_nt(attn_grad_full, output_full).astype(jnp.bfloat16)
    grad_heads = context_grad.reshape(seq_len, local_heads, HD)
    scores = masked_scores(query_heads, key_heads, key_valid, score_scale)
    attn_probs = jnp.exp(scores - log_total)
    probs_low = attn_probs.astype(jnp.bfloat16)
    prob_grad = jnp.einsum(
        "qhd,khd->hqk", grad_heads, value_heads, preferred_element_type=jnp.float32
    )
    row_inner = jnp.sum(attn_probs * prob_grad, axis=-1, keepdims=True)
    score_grad = (attn_probs * (prob_grad - row_inner) * score_scale).astype(jnp.bfloat16)
    query_parts = jnp.einsum(
        "hqk,khd->qhd", score_grad, key_heads, preferred_element_type=jnp.float32
    )
    key_total = jnp.einsum(
        "hqk,qhd->khd", score_grad, query_heads, preferred_element_type=jnp.float32
    )
    value_total = jnp.einsum(
        "hqk,qhd->khd", probs_low, grad_heads, preferred_element_type=jnp.float32
    )
    query_grad = query_parts.reshape(seq_len, local_width)
    key_grad = key_total.reshape(seq_len, local_width)
    value_grad = value_total.reshape(seq_len, local_width)
    grad_query_bias = jnp.sum(query_grad, axis=0)
    grad_value_bias = jnp.sum(value_grad, axis=0)
    query_low = query_grad.astype(jnp.bfloat16)
    key_low = key_grad.astype(jnp.bfloat16)
    value_low = value_grad.astype(jnp.bfloat16)
    grad_query = matmul_tn(hidden_full, query_low)
    grad_key = matmul_tn(hidden_full, key_low)
    grad_value = matmul_tn(hidden_full, value_low)
    grad_in = (
        first_grad
        + lax.psum_scatter(
            (
                matmul_nt(query_low, query_full)
                + matmul_nt(key_low, key_full)
                + matmul_nt(value_low, value_full)
            ).astype(jnp.bfloat16),
            "tensor",
            scatter_dimension=0,
            tiled=True,
        ).astype(jnp.float32)
    ).astype(jnp.bfloat16)
    owned_rows = (
        lax.psum_scatter(grad_query, "dp", scatter_dimension=0, tiled=True),
        lax.psum_scatter(grad_key, "dp", scatter_dimension=0, tiled=True),
        lax.psum_scatter(grad_value, "dp", scatter_dimension=0, tiled=True),
        lax.psum_scatter(grad_up, "dp", scatter_dimension=0, tiled=True),
    )
    owned_cols = (
        lax.psum_scatter(grad_output, "dp", scatter_dimension=1, tiled=True),
        lax.psum_scatter(grad_down, "dp", scatter_dimension=1, tiled=True),
    )
    summed = lax.psum(
        (
            widen(grad_query_bias, tensor_index, n_tensor),
            widen(grad_value_bias, tensor_index, n_tensor),
            widen(grad_up_bias, tensor_index, n_tensor),
            grad_output_bias,
            grad_down_bias,
            grad_first_gain,
            grad_first_shift,
            grad_second_gain,
            grad_second_shift,
        ),
        ("dp", "tensor"),
    )
    local_ff = up_weight.shape[1]
    query_bias_grad = lax.dynamic_slice_in_dim(
        summed[0], tensor_index * local_width, local_width, 0
    )
    value_bias_grad = lax.dynamic_slice_in_dim(
        summed[1], tensor_index * local_width, local_width, 0
    )
    up_bias_grad = lax.dynamic_slice_in_dim(summed[2], tensor_index * local_ff, local_ff, 0)
    return (
        hidden_out,
        grad_in,
        owned_rows[0],
        owned_rows[1],
        owned_rows[2],
        owned_cols[0],
        owned_rows[3],
        owned_cols[1],
        query_bias_grad,
        value_bias_grad,
        summed[3],
        up_bias_grad,
        summed[4],
        summed[5],
        summed[6],
        summed[7],
        summed[8],
    )


def solution(mesh):
    in_specs = (
        P(("dp", "tensor"), None),
        P(("dp", "tensor"), None),
        P("dp"),
        P("dp", "tensor"),
        P("dp", "tensor"),
        P("dp", "tensor"),
        P("tensor", "dp"),
        P("dp", "tensor"),
        P("tensor", "dp"),
        P("tensor"),
        P("tensor"),
        P(),
        P("tensor"),
        P(),
        P(),
        P(),
        P(),
        P(),
    )
    out_specs = (
        P(("dp", "tensor"), None),
        P(("dp", "tensor"), None),
        P("dp", "tensor"),
        P("dp", "tensor"),
        P("dp", "tensor"),
        P("tensor", "dp"),
        P("dp", "tensor"),
        P("tensor", "dp"),
        P("tensor"),
        P("tensor"),
        P(),
        P("tensor"),
        P(),
        P(),
        P(),
        P(),
        P(),
    )
    return jax.shard_map(shards, mesh=mesh, in_specs=in_specs, out_specs=out_specs, check_vma=False)
```

profile of v0, /device:TPU:0, one launch (start us, length us, event | category | flops | bytes accessed | tf_op | source)
XLA Modules:
  0.0 855.3 jit_solution(8635387933695956339)
XLA Ops:
  9.5 33.4 %all_gather.32 = bf16[1024,256]{1,0:T(8,128)(2,1)S(1)} all-gather(bf16[128,256]{1,0:T(8,128)(2,1)} %param.21), channel_id=1, replica_groups=mesh['dp'=8,'tensor'=4] {'dp'}, dimensions={0}, use_global_device_ids=true | all-gather | bytes 589824 | tf_op jit(solution)/shard_map/all_gather | solution.py:58
  42.8 31.6 %all_gather.33 = bf16[1024,256]{1,0:T(8,128)(2,1)S(1)} all-gather(bf16[128,256]{1,0:T(8,128)(2,1)} %param.22), channel_id=1, replica_groups=mesh['dp'=8,'tensor'=4] {'dp'}, dimensions={0}, use_global_device_ids=true | all-gather | bytes 589824 | tf_op jit(solution)/shard_map/all_gather | solution.py:59
  74.5 31.8 %all_gather.31 = bf16[1024,256]{1,0:T(8,128)(2,1)S(1)} all-gather(bf16[128,256]{1,0:T(8,128)(2,1)} %param.23), channel_id=1, replica_groups=mesh['dp'=8,'tensor'=4] {'dp'}, dimensions={0}, use_global_device_ids=true | all-gather | bytes 589824 | tf_op jit(solution)/shard_map/all_gather | solution.py:60
  106.3 27.2 %all_gather.34 = bf16[256,1024]{1,0:T(8,128)(2,1)S(1)} all-gather(bf16[256,128]{1,0:T(8,128)(2,1)} %param.24), channel_id=1, replica_groups=mesh['dp'=8,'tensor'=4] {'dp'}, dimensions={1}, use_global_device_ids=true | all-gather | bytes 589824 | tf_op jit(solution)/shard_map/all_gather | solution.py:64
  143.8 23.5 %reduce-scatter.11.cloned.1.call-done = bf16[128,1024]{1,0:T(8,128)(2,1)} async-done(((bf16[512,1024]{1,0:T(8,128)(2,1)}), bf16[128,1024]{1,0:T(8,128)(2,1)}) %reduce-scatter.11.cloned.1.call-update) | async-done | bytes 262160 | tf_op jit(solution)/shard_map/reduce_scatter | solution.py:133
  172.1 21.9 %all-gather.11.cloned.1.call-done = bf16[1024,1024]{1,0:T(8,128)(2,1)} async-done(((bf16[128,1024]{1,0:T(8,128)(2,1)}), bf16[1024,1024]{1,0:T(8,128)(2,1)}) %all-gather.11.cloned.1.call-update) | async-done | bytes 2097168 | tf_op jit(solution)/shard_map/all_gather | solution.py:61
  194.0 17.2 %all-gather.9.cloned.1.call-done = bf16[512,1024]{1,0:T(8,128)(2,1)} async-done(((bf16[128,1024]{1,0:T(8,128)(2,1)}), bf16[512,1024]{1,0:T(8,128)(2,1)}) %all-gather.9.cloned.1.call-update) | async-done | bytes 1048592 | tf_op jit(solution)/shard_map/all_gather | solution.py:139
  211.2 4.9 multiply_convert_fusion.1
  216.1 47.5 %all-gather.13.cloned.1.call-done = bf16[1024,1024]{1,0:T(8,128)(2,1)} async-done(((bf16[1024,128]{1,0:T(8,128)(2,1)}), bf16[1024,1024]{1,0:T(8,128)(2,1)}) %all-gather.13.cloned.1.call-update) | async-done | bytes 2097168 | tf_op jit(solution)/shard_map/all_gather | solution.py:65
  267.9 23.1 %reduce-scatter.13.cloned.1.call-done = bf16[128,1024]{1,0:T(8,128)(2,1)} async-done(((bf16[512,1024]{1,0:T(8,128)(2,1)}), bf16[128,1024]{1,0:T(8,128)(2,1)}) %reduce-scatter.13.cloned.1.call-update) | async-done | bytes 262160 | tf_op jit(solution)/shard_map/reduce_scatter | solution.py:142
  294.1 16.6 %all-gather.15.cloned.1.call-done = bf16[512,1024]{1,0:T(8,128)(2,1)} async-done(((bf16[128,1024]{1,0:T(8,128)(2,1)}), bf16[512,1024]{1,0:T(8,128)(2,1)}) %all-gather.15.cloned.1.call-update) | async-done | bytes 1048592 | tf_op jit(solution)/shard_map/all_gather | solution.py:154
  310.7 4.6 fusion.53
  318.7 24.9 %reduce-scatter.15.cloned.1.call-done = bf16[128,1024]{1,0:T(8,128)(2,1)} async-done(((bf16[512,1024]{1,0:T(8,128)(2,1)}), bf16[128,1024]{1,0:T(8,128)(2,1)}) %reduce-scatter.15.cloned.1.call-update) | async-done | bytes 262160 | tf_op jit(solution)/shard_map/reduce_scatter | solution.py:160
  347.0 16.6 %all-gather.17.cloned.1.call-done = bf16[512,1024]{1,0:T(8,128)(2,1)} async-done(((bf16[128,1024]{1,0:T(8,128)(2,1)}), bf16[512,1024]{1,0:T(8,128)(2,1)}) %all-gather.17.cloned.1.call-update) | async-done | bytes 1048592 | tf_op jit(solution)/shard_map/all_gather | solution.py:168
  373.2 8.5 fusion.23
  383.2 9.1 %fusion.50 = (f32[4,64]{1,0:T(4,128)S(1)}, bf16[512,4,64]{0,2,1:T(8,128)(2,1)}) fusion(bf16[512,4,64]{0,2,1:T(8,128)(2,1)S(1)} %bitcast.71, f32[4,512,512]{1,2,0:T(8,128)} %fusion.54, f32[4,512]{1,0:T(4,128)S(1)} %log_add_fusion, f32[4,512,512]{1,2,0:T(8,128)} %copy-done.1, pred[512]{0:T(512)(128)(4,1)S(1)} %iota_compare_fusion), kind=kOutput, calls=%fused_computation.87 | convolution fusion | flops 146016512 | bytes 8922624 | tf_op jit(solution)/shard_map/hqk,khd->qhd/dot_general | solution.py:180
  402.4 4.5 fusion.58
  412.3 40.8 %all-reduce = (f32[1024]{0:T(1024)S(1)}, f32[1024]{0:T(1024)S(1)}, f32[1024]{0:T(1024)}, f32[4096]{0:T(1024)S(1)}, f32[1024]{0:T(1024)}, /*index=5*/f32[1024]{0:...) all-reduce(f32[1024]{0:T(1024)S(1)} %dynamic_update_slice.9, ...), channel_id=1, replica_groups=mesh['dp'=8,'tensor'=4] {'dp','tensor'}, use_global_device_ids=true, to_apply=%region_22.23 | all-reduce | flops 12288 | bytes 98304 | tf_op jit(solution)/shard_map/psum | solution.py:223
  456.6 45.8 %reduce-scatter.21.cloned.1.call-done = f32[128,256]{0,1:T(8,128)} async-done(((f32[1024,256]{0,1:T(8,128)}), f32[128,256]{0,1:T(8,128)}) %reduce-scatter.21.cloned.1.call-update) | async-done | bytes 131088 | tf_op jit(solution)/shard_map/reduce_scatter | solution.py:215
  504.1 65.3 %reduce-scatter.19.cloned.1.call-done = f32[128,256]{0,1:T(8,128)} async-done(((f32[1024,256]{0,1:T(8,128)}), f32[128,256]{0,1:T(8,128)}) %reduce-scatter.19.cloned.1.call-update) | async-done | bytes 131088 | tf_op jit(solution)/shard_map/reduce_scatter | solution.py:214
  571.1 24.5 %reduce-scatter.17.cloned.1.call-done = bf16[128,1024]{1,0:T(8,128)(2,1)} async-done(((bf16[512,1024]{1,0:T(8,128)(2,1)}), bf16[128,1024]{1,0:T(8,128)(2,1)}) %reduce-scatter.17.cloned.1.call-update) | async-done | bytes 262160 | tf_op jit(solution)/shard_map/reduce_scatter | solution.py:202
  597.3 66.8 %reduce-scatter.25.cloned.1.call-done = f32[256,128]{1,0:T(8,128)} async-done(((f32[256,1024]{1,0:T(8,128)}), f32[256,128]{1,0:T(8,128)}) %reduce-scatter.25.cloned.1.call-update) | async-done | bytes 131088 | tf_op jit(solution)/shard_map/reduce_scatter | solution.py:220
  664.1 91.9 %reduce-scatter.29.cloned.1.call-done = f32[1024,128]{1,0:T(8,128)} async-done(((f32[1024,1024]{1,0:T(8,128)}), f32[1024,128]{1,0:T(8,128)}) %reduce-scatter.29.cloned.1.call-update) | async-done | bytes 524304 | tf_op jit(solution)/shard_map/reduce_scatter | solution.py:221
  756.0 91.9 %reduce-scatter.27.cloned.1.call-done = f32[128,1024]{1,0:T(8,128)} async-done(((f32[1024,1024]{1,0:T(8,128)}), f32[128,1024]{1,0:T(8,128)}) %reduce-scatter.27.cloned.1.call-update) | async-done | bytes 524304 | tf_op jit(solution)/shard_map/reduce_scatter | solution.py:217
  (154 shorter events, 64.6 us)
Async XLA Ops:
  8.0 127.4 %copy-start.31 = (f32[256]{0:T(256)S(1)}, f32[256]{0:T(256)}, u32[]{:S(2)}) copy-start(f32[256]{0:T(256)} %param.27) | copy-start | bytes 3076
  8.0 125.5 %all-gather.7.cloned.1.call-start = ((), (), s32[]{:S(2)}) async-start(), calls=%async_computation.10 | async-start | bytes 1310720 | tf_op jit(solution)/shard_map/all_gather | solution.py:117
  8.8 158.6 %reduce-scatter.11.cloned.1.call-start = ((), (), s32[]{:S(2)}) async-start(), calls=%async_computation.11 | async-start | bytes 1310720 | tf_op jit(solution)/shard_map/reduce_scatter | solution.py:133
  42.8 94.4 %copy-start.7 = (bf16[1024,256]{1,0:T(8,128)(2,1)}, bf16[1024,256]{1,0:T(8,128)(2,1)S(1)}, u32[]{:S(2)}) copy-start(bf16[1024,256]{1,0:T(8,128)(2,1)S(1)} %all_gather.32) | copy-start | bytes 1572868
  106.3 33.7 %copy-start.4 = (bf16[1024,256]{1,0:T(8,128)(2,1)}, bf16[1024,256]{1,0:T(8,128)(2,1)S(1)}, u32[]{:S(2)}) copy-start(bf16[1024,256]{1,0:T(8,128)(2,1)S(1)} %all_gather.31) | copy-start | bytes 1572868
  140.5 29.1 %copy-start.24 = (f32[1024]{0:T(1024)S(1)}, f32[1024]{0:T(1024)}, u32[]{:S(2)}) copy-start(f32[1024]{0:T(1024)} %param.32) | copy-start | bytes 12292
  141.6 69.5 %copy-start.30 = (f32[1024]{0:T(1024)S(1)}, f32[1024]{0:T(1024)}, u32[]{:S(2)}) copy-start(f32[1024]{0:T(1024)} %param.30) | copy-start | bytes 12292
  143.2 50.8 %all-gather.11.cloned.1.call-start = ((), (), s32[]{:S(2)}) async-start(), calls=%async_computation.13 | async-start | bytes 2359296 | tf_op jit(solution)/shard_map/all_gather | solution.py:61
  143.7 67.4 %all-gather.9.cloned.1.call-start = ((), (), s32[]{:S(2)}) async-start(), calls=%async_computation.12 | async-start | bytes 1310720 | tf_op jit(solution)/shard_map/all_gather | solution.py:139
  171.5 92.1 %all-gather.13.cloned.1.call-start = ((), (), s32[]{:S(2)}) async-start(), calls=%async_computation.14 | async-start | bytes 2359296 | tf_op jit(solution)/shard_map/all_gather | solution.py:65
  172.1 118.9 %reduce-scatter.13.cloned.1.call-start = ((), (), s32[]{:S(2)}) async-start(), calls=%async_computation.15 | async-start | bytes 1310720 | tf_op jit(solution)/shard_map/reduce_scatter | solution.py:142
  216.1 74.9 %copy-start.3 = (bf16[128,1024]{1,0:T(8,128)(2,1)S(1)}, bf16[128,1024]{1,0:T(8,128)(2,1)}, u32[]{:S(2)}) copy-start(bf16[128,1024]{1,0:T(8,128)(2,1)} %reduce-scatter.11.cloned.1.call-done) | copy-start | bytes 786436
  216.1 74.9 %copy-start.27 = (f32[1024]{0:T(1024)S(1)}, f32[1024]{0:T(1024)}, u32[]{:S(2)}) copy-start(f32[1024]{0:T(1024)} %param.31) | copy-start | bytes 12292
  263.6 29.2 %copy-start.28 = (f32[1024]{0:T(1024)S(1)}, f32[1024]{0:T(1024)}, u32[]{:S(2)}) copy-start(f32[1024]{0:T(1024)} %param.35) | copy-start | bytes 12292
  267.8 42.9 %all-gather.15.cloned.1.call-start = ((), (), s32[]{:S(2)}) async-start(), calls=%async_computation.16 | async-start | bytes 1310720 | tf_op jit(solution)/shard_map/all_gather | solution.py:154
  293.9 49.7 %reduce-scatter.15.cloned.1.call-start = ((), (), s32[]{:S(2)}) async-start(), calls=%async_computation.17 | async-start | bytes 1310720 | tf_op jit(solution)/shard_map/reduce_scatter | solution.py:160
  318.7 45.0 %all-gather.17.cloned.1.call-start = ((), (), s32[]{:S(2)}) async-start(), calls=%async_computation.18 | async-start | bytes 1310720 | tf_op jit(solution)/shard_map/all_gather | solution.py:168
  347.0 108.0 %reduce-scatter.23.cloned.1.call-start = ((), (), s32[]{:S(2)}) async-start(), calls=%async_computation.22 | async-start | bytes 1179648 | tf_op jit(solution)/shard_map/reduce_scatter | solution.py:216
  370.4 132.1 %reduce-scatter.21.cloned.1.call-start = ((), (), s32[]{:S(2)}) async-start(), calls=%async_computation.21 | async-start | bytes 1179648 | tf_op jit(solution)/shard_map/reduce_scatter | solution.py:215
  383.1 186.3 %reduce-scatter.19.cloned.1.call-start = ((), (), s32[]{:S(2)}) async-start(), calls=%async_computation.20 | async-start | bytes 1179648 | tf_op jit(solution)/shard_map/reduce_scatter | solution.py:214
  394.8 200.8 %reduce-scatter.17.cloned.1.call-start = ((), (), s32[]{:S(2)}) async-start(), calls=%async_computation.19 | async-start | bytes 1310720 | tf_op jit(solution)/shard_map/reduce_scatter | solution.py:202
  399.5 264.6 %reduce-scatter.25.cloned.1.call-start = ((), (), s32[]{:S(2)}) async-start(), calls=%async_computation.23 | async-start | bytes 1179648 | tf_op jit(solution)/shard_map/reduce_scatter | solution.py:220
  402.4 353.6 %reduce-scatter.29.cloned.1.call-start = ((), (), s32[]{:S(2)}) async-start(), calls=%async_computation.25 | async-start | bytes 4718592 | tf_op jit(solution)/shard_map/reduce_scatter | solution.py:221
  407.0 440.9 %reduce-scatter.27.cloned.1.call-start = ((), (), s32[]{:S(2)}) async-start(), calls=%async_computation.24 | async-start | bytes 4718592 | tf_op jit(solution)/shard_map/reduce_scatter | solution.py:217
  (25 other events, 223.3 us)
Sparse Core Ops, SparseCore 0:
  10.4 19.4 all-gather.6
  143.3 24.0 reduce-scatter.10
  268.0 22.9 reduce-scatter.12
  294.0 16.6 all-gather.14
  318.8 24.7 reduce-scatter.14
Sparse Core Ops, SparseCore 1:
  145.8 48.2 all-gather.10
  196.0 15.1 all-gather.8
  213.1 50.4 all-gather.12
  347.0 16.5 all-gather.16
  370.5 64.9 reduce-scatter.22
  438.8 63.6 reduce-scatter.20
  505.7 63.6 reduce-scatter.18
  571.8 23.7 reduce-scatter.16
  599.4 64.6 reduce-scatter.24
  668.4 87.6 reduce-scatter.28
  760.1 87.8 reduce-scatter.26
where the time goes:
time: 856 us; the launch traced here: 855 us
  waiting for transfers between devices  580 us (68%)
  blocking collectives  165 us (19%)
  matrix products  69.6 us (8%)
  between operations  16.7 us (2%)
  other arithmetic  12.9 us (2%)
  local copies, waits for them, and re-layouts  10.7 us (1%)
    reduce_scatter x1, waiting for transfers between devices, shards(): lax.psum_scatter(grad_up, 'dp', scatter_dimension=0, tiled=True)  91.9 us
    reduce_scatter x1, waiting for transfers between devices, shards(): lax.psum_scatter(grad_down, 'dp', scatter_dimension=1, tiled=True)  91.9 us
    reduce_scatter x1, waiting for transfers between devices, shards(): lax.psum_scatter(grad_output, 'dp', scatter_dimension=1, tiled=True)  66.8 us
    reduce_scatter x1, waiting for transfers between devices, shards(): lax.psum_scatter(grad_query, 'dp', scatter_dimension=0, tiled=True)  65.3 us
    all_gather x1, waiting for transfers between devices, fetch_weights(): lax.all_gather(down_weight, 'dp', axis=1, tiled=True)  47.5 us
    reduce_scatter x1, waiting for transfers between devices, shards(): lax.psum_scatter(grad_key, 'dp', scatter_dimension=0, tiled=True)  45.8 us
    psum x1, blocking collectives, shards(): lax.psum((widen(grad_query_bias, tensor_index, n_tensor), widen(grad_valu...  40.8 us
    all_gather x1, blocking collectives, fetch_weights(): lax.all_gather(query_weight, 'dp', axis=0, tiled=True)  33.4 us
  transfers between devices with their start and end apart: 16, of which 14 were waited for; matrix products, arithmetic and copies ran while one was open for 7% of the time, Pallas kernels for 0%

commit v1 on v0

--- a/solution.py
+++ b/solution.py
@@ -8,6 +8,19 @@
 ROOT_HALF = 0.7071067811865476
 INV_ROOT_TWO_PI = 0.3989422804014327
 MASKED = -1e30
+
+
+def gather_around(array, axis, dim):
+    size, position, rows = (lax.axis_size(axis), lax.axis_index(axis), array.shape[dim])
+    upward = [(i, (i + 1) % size) for i in range(size)]
+    out = jnp.zeros((*array.shape[:dim], size * rows, *array.shape[dim + 1 :]), array.dtype)
+    carried = array
+    for hop in range(size):
+        holder = (position - hop) % size
+        out = lax.dynamic_update_slice_in_dim(out, carried, holder * rows, axis=dim)
+        if hop < size - 1:
+            carried = lax.ppermute(carried, axis, upward)
+    return out
 
 
 def matmul(left_side, right_side):
@@ -62,7 +75,7 @@
     )
     col_parts = (
         lax.all_gather(output_weight, "dp", axis=1, tiled=True),
-        lax.all_gather(down_weight, "dp", axis=1, tiled=True),
+        gather_around(down_weight, "dp", 1),
     )
     return (row_parts, col_parts)
 

time: 856 us -> 827 us (0.966)
  waiting for transfers between devices: 580 us -> 540 us
  local copies, waits for them, and re-layouts: 10.7 us -> 20.3 us
    ppermute x0 -> x7, waiting for transfers between devices: none -> 71 us  [gather_around(): carried = lax.ppermute(carried, axis, upward)]
    all_gather x1 -> x0, waiting for transfers between devices: 47.5 us -> none  [fetch_weights(): lax.all_gather(down_weight, 'dp', axis=1, tiled=True)]
    reduce_scatter x1, waiting for transfers between devices: 23.5 us -> 0.01 us  [shards(): lax.psum_scatter(matmul(context, output_full).astype(jnp.bfloat16), 'tens...]
    all_gather x1, waiting for transfers between devices: 21.9 us -> 0.01 us  [fetch_weights(): lax.all_gather(up_weight, 'dp', axis=0, tiled=True)]
    all_gather x1, waiting for transfers between devices: 17.2 us -> 0.01 us  [shards(): normed_full = lax.all_gather(first_low, 'tensor', axis=0, tiled=True)]
  transfers between devices with their start and end apart: 16 -> 22, of which waited for: 14 -> 17; matrix products, arithmetic and copies ran while one was open for 7% -> 7% of each run, Pallas kernels for 0% -> 0%
where the time goes in v1:
time: 827 us; the launch traced here: 826 us
  waiting for transfers between devices  540 us (65%)
  blocking collectives  165 us (20%)
  matrix products  67.5 us (8%)
  local copies, waits for them, and re-layouts  20.3 us (2%)
  between operations  16.7 us (2%)
  other arithmetic  12.9 us (2%)
    reduce_scatter x1, waiting for transfers between devices, shards(): lax.psum_scatter(grad_down, 'dp', scatter_dimension=1, tiled=True)  91.9 us
    reduce_scatter x1, waiting for transfers between devices, shards(): lax.psum_scatter(grad_up, 'dp', scatter_dimension=0, tiled=True)  91.9 us
    ppermute x7, waiting for transfers between devices, gather_around(): carried = lax.ppermute(carried, axis, upward)  71 us
    reduce_scatter x1, waiting for transfers between devices, shards(): lax.psum_scatter(grad_output, 'dp', scatter_dimension=1, tiled=True)  66.9 us
    reduce_scatter x1, waiting for transfers between devices, shards(): lax.psum_scatter(grad_query, 'dp', scatter_dimension=0, tiled=True)  65.4 us
    reduce_scatter x1, waiting for transfers between devices, shards(): lax.psum_scatter(grad_key, 'dp', scatter_dimension=0, tiled=True)  47.2 us
    psum x1, blocking collectives, shards(): lax.psum((widen(grad_query_bias, tensor_index, n_tensor), widen(grad_valu...  40.9 us
    all_gather x1, blocking collectives, fetch_weights(): lax.all_gather(query_weight, 'dp', axis=0, tiled=True)  33.4 us
  transfers between devices with their start and end apart: 22, of which 17 were waited for; matrix products, arithmetic and copies ran while one was open for 7% of the time, Pallas kernels for 0%

profile of v1, /device:TPU:0, one launch (start us, length us, event | category | flops | bytes accessed | tf_op | source)
XLA Modules:
  0.0 826.1 jit_solution(3894954953680938913)
XLA Ops:
  9.5 33.4 %all_gather.29 = bf16[1024,256]{1,0:T(8,128)(2,1)S(1)} all-gather(bf16[128,256]{1,0:T(8,128)(2,1)} %param.21), channel_id=1, replica_groups=mesh['dp'=8,'tensor'=4] {'dp'}, dimensions={0}, use_global_device_ids=true | all-gather | bytes 589824 | tf_op jit(solution)/shard_map/all_gather | solution.py:71
  42.8 31.6 %all_gather.30 = bf16[1024,256]{1,0:T(8,128)(2,1)S(1)} all-gather(bf16[128,256]{1,0:T(8,128)(2,1)} %param.22), channel_id=1, replica_groups=mesh['dp'=8,'tensor'=4] {'dp'}, dimensions={0}, use_global_device_ids=true | all-gather | bytes 589824 | tf_op jit(solution)/shard_map/all_gather | solution.py:72
  74.5 31.8 %all_gather.28 = bf16[1024,256]{1,0:T(8,128)(2,1)S(1)} all-gather(bf16[128,256]{1,0:T(8,128)(2,1)} %param.23), channel_id=1, replica_groups=mesh['dp'=8,'tensor'=4] {'dp'}, dimensions={0}, use_global_device_ids=true | all-gather | bytes 589824 | tf_op jit(solution)/shard_map/all_gather | solution.py:73
  106.3 27.2 %all_gather.31 = bf16[256,1024]{1,0:T(8,128)(2,1)S(1)} all-gather(bf16[256,128]{1,0:T(8,128)(2,1)} %param.24), channel_id=1, replica_groups=mesh['dp'=8,'tensor'=4] {'dp'}, dimensions={1}, use_global_device_ids=true | all-gather | bytes 589824 | tf_op jit(solution)/shard_map/all_gather | solution.py:77
  146.0 6.9 collective-permute-done
  152.9 14.5 %collective-permute-done.1 = bf16[1024,128]{1,0:T(8,128)(2,1)S(1)} collective-permute-done((bf16[1024,128]{1,0:T(8,128)(2,1)S(1)}, bf16[1024,128]{1,0:T(8,128)(2,1)S(1)}, u32[]{:S(2)}, u32[]{:S(2)}) %collective-permute-start.1) | collective-permute-done | bytes 262176 | tf_op jit(solution)/shard_map/ppermute | solution.py:22
  171.5 4.9 collective-permute-done.2
  176.4 16.7 %collective-permute-done.3 = bf16[1024,128]{1,0:T(8,128)(2,1)S(1)} collective-permute-done((bf16[1024,128]{1,0:T(8,128)(2,1)S(1)}, bf16[1024,128]{1,0:T(8,128)(2,1)S(1)}, u32[]{:S(2)}, u32[]{:S(2)}) %collective-permute-start.3) | collective-permute-done | bytes 262176 | tf_op jit(solution)/shard_map/ppermute | solution.py:22
  195.5 13.2 %collective-permute-done.4 = bf16[1024,128]{1,0:T(8,128)(2,1)} collective-permute-done((bf16[1024,128]{1,0:T(8,128)(2,1)S(1)}, bf16[1024,128]{1,0:T(8,128)(2,1)}, u32[]{:S(2)}, u32[]{:S(2)}) %collective-permute-start.4) | collective-permute-done | bytes 262176 | tf_op jit(solution)/shard_map/ppermute | solution.py:22
  211.0 9.1 %collective-permute-done.5 = bf16[1024,128]{1,0:T(8,128)(2,1)S(1)} collective-permute-done((bf16[1024,128]{1,0:T(8,128)(2,1)}, bf16[1024,128]{1,0:T(8,128)(2,1)S(1)}, u32[]{:S(2)}, u32[]{:S(2)}) %collective-permute-start.5) | collective-permute-done | bytes 262176 | tf_op jit(solution)/shard_map/ppermute | solution.py:22
  223.3 5.8 collective-permute-done.6
  239.5 22.3 %reduce-scatter.13.cloned.1.call-done = bf16[128,1024]{1,0:T(8,128)(2,1)} async-done(((bf16[512,1024]{1,0:T(8,128)(2,1)}), bf16[128,1024]{1,0:T(8,128)(2,1)}) %reduce-scatter.13.cloned.1.call-update) | async-done | bytes 262160 | tf_op jit(solution)/shard_map/reduce_scatter | solution.py:155
  264.9 16.4 %all-gather.12.cloned.1.call-done = bf16[512,1024]{1,0:T(8,128)(2,1)} async-done(((bf16[128,1024]{1,0:T(8,128)(2,1)}), bf16[512,1024]{1,0:T(8,128)(2,1)}) %all-gather.12.cloned.1.call-update) | async-done | bytes 1048592 | tf_op jit(solution)/shard_map/all_gather | solution.py:167
  289.3 24.9 %reduce-scatter.15.cloned.1.call-done = bf16[128,1024]{1,0:T(8,128)(2,1)} async-done(((bf16[512,1024]{1,0:T(8,128)(2,1)}), bf16[128,1024]{1,0:T(8,128)(2,1)}) %reduce-scatter.15.cloned.1.call-update) | async-done | bytes 262160 | tf_op jit(solution)/shard_map/reduce_scatter | solution.py:173
  317.6 16.6 %all-gather.14.cloned.1.call-done = bf16[512,1024]{1,0:T(8,128)(2,1)} async-done(((bf16[128,1024]{1,0:T(8,128)(2,1)}), bf16[512,1024]{1,0:T(8,128)(2,1)}) %all-gather.14.cloned.1.call-update) | async-done | bytes 1048592 | tf_op jit(solution)/shard_map/all_gather | solution.py:181
  343.8 8.5 %fusion.23 = bf16[4,64,512]{2,1,0:T(8,128)(2,1)S(1)} fusion(bf16[512,4,64]{0,2,1:T(8,128)(2,1)S(1)} %bitcast.79, f32[4,512,512]{1,2,0:T(8,128)} %fusion.54, f32[4,512,512]{1,2,0:T(8,128)} %copy-done.1, f32[4,512]{1,0:T(4,128)S(1)} %log_add_fusion, pred[512]{0:T(512)(128)(4,1)S(1)} %iota_compare_fusion), kind=kOutput, calls=%fused_computation.33 | convolution fusion | flops 145885696 | bytes 8921600 | tf_op jit(solution)/shard_map/hqk,qhd->khd/dot_general | solution.py:196
  353.8 9.1 %fusion.50 = (f32[4,64]{1,0:T(4,128)S(1)}, bf16[512,4,64]{0,2,1:T(8,128)(2,1)}) fusion(bf16[512,4,64]{0,2,1:T(8,128)(2,1)S(1)} %bitcast.71, f32[4,512,512]{1,2,0:T(8,128)} %fusion.54, f32[4,512]{1,0:T(4,128)S(1)} %log_add_fusion, f32[4,512,512]{1,2,0:T(8,128)} %copy-done.1, pred[512]{0:T(512)(128)(4,1)S(1)} %iota_compare_fusion), kind=kOutput, calls=%fused_computation.95 | convolution fusion | flops 146016512 | bytes 8922624 | tf_op jit(solution)/shard_map/hqk,khd->qhd/dot_general | solution.py:193
  381.6 40.9 %all-reduce = (f32[1024]{0:T(1024)S(1)}, f32[1024]{0:T(1024)S(1)}, f32[1024]{0:T(1024)}, f32[4096]{0:T(1024)S(1)}, f32[1024]{0:T(1024)}, /*index=5*/f32[1024]{0:...) all-reduce(f32[1024]{0:T(1024)S(1)} %dynamic_update_slice.41, ...), channel_id=1, replica_groups=mesh['dp'=8,'tensor'=4] {'dp','tensor'}, use_global_device_ids=true, to_apply=%region_22.23 | all-reduce | flops 12288 | bytes 98304 | tf_op jit(solution)/shard_map/psum | solution.py:236
  426.0 47.2 %reduce-scatter.21.cloned.1.call-done = f32[128,256]{0,1:T(8,128)} async-done(((f32[1024,256]{0,1:T(8,128)}), f32[128,256]{0,1:T(8,128)}) %reduce-scatter.21.cloned.1.call-update) | async-done | bytes 131088 | tf_op jit(solution)/shard_map/reduce_scatter | solution.py:228
  474.8 65.4 %reduce-scatter.19.cloned.1.call-done = f32[128,256]{0,1:T(8,128)} async-done(((f32[1024,256]{0,1:T(8,128)}), f32[128,256]{0,1:T(8,128)}) %reduce-scatter.19.cloned.1.call-update) | async-done | bytes 131088 | tf_op jit(solution)/shard_map/reduce_scatter | solution.py:227
  541.8 24.5 %reduce-scatter.17.cloned.1.call-done = bf16[128,1024]{1,0:T(8,128)(2,1)} async-done(((bf16[512,1024]{1,0:T(8,128)(2,1)}), bf16[128,1024]{1,0:T(8,128)(2,1)}) %reduce-scatter.17.cloned.1.call-update) | async-done | bytes 262160 | tf_op jit(solution)/shard_map/reduce_scatter | solution.py:215
  568.1 66.9 %reduce-scatter.25.cloned.1.call-done = f32[256,128]{1,0:T(8,128)} async-done(((f32[256,1024]{1,0:T(8,128)}), f32[256,128]{1,0:T(8,128)}) %reduce-scatter.25.cloned.1.call-update) | async-done | bytes 131088 | tf_op jit(solution)/shard_map/reduce_scatter | solution.py:233
  634.9 91.9 %reduce-scatter.29.cloned.1.call-done = f32[1024,128]{1,0:T(8,128)} async-done(((f32[1024,1024]{1,0:T(8,128)}), f32[1024,128]{1,0:T(8,128)}) %reduce-scatter.29.cloned.1.call-update) | async-done | bytes 524304 | tf_op jit(solution)/shard_map/reduce_scatter | solution.py:234
  726.9 91.9 %reduce-scatter.27.cloned.1.call-done = f32[128,1024]{1,0:T(8,128)} async-done(((f32[1024,1024]{1,0:T(8,128)}), f32[128,1024]{1,0:T(8,128)}) %reduce-scatter.27.cloned.1.call-update) | async-done | bytes 524304 | tf_op jit(solution)/shard_map/reduce_scatter | solution.py:230
  (176 shorter events, 87.9 us)
Async XLA Ops:
  8.0 127.4 %copy-start.32 = (f32[256]{0:T(256)S(1)}, f32[256]{0:T(256)}, u32[]{:S(2)}) copy-start(f32[256]{0:T(256)} %param.27) | copy-start | bytes 3076
  8.0 125.5 %all-gather.6.cloned.1.call-start = ((), (), s32[]{:S(2)}) async-start(), calls=%async_computation.10 | async-start | bytes 1310720 | tf_op jit(solution)/shard_map/all_gather | solution.py:130
  8.8 158.6 %reduce-scatter.11.cloned.1.call-start = ((), (), s32[]{:S(2)}) async-start(), calls=%async_computation.11 | async-start | bytes 1310720 | tf_op jit(solution)/shard_map/reduce_scatter | solution.py:146
  42.8 94.3 %copy-start.7 = (bf16[1024,256]{1,0:T(8,128)(2,1)}, bf16[1024,256]{1,0:T(8,128)(2,1)S(1)}, u32[]{:S(2)}) copy-start(bf16[1024,256]{1,0:T(8,128)(2,1)S(1)} %all_gather.29) | copy-start | bytes 1572868
  143.1 86.7 %all-gather.10.cloned.1.call-start = ((), (), s32[]{:S(2)}) async-start(), calls=%async_computation.13 | async-start | bytes 2359296 | tf_op jit(solution)/shard_map/all_gather | solution.py:74
  143.7 86.2 %all-gather.8.cloned.1.call-start = ((), (), s32[]{:S(2)}) async-start(), calls=%async_computation.12 | async-start | bytes 1310720 | tf_op jit(solution)/shard_map/all_gather | solution.py:152
  143.7 9.1 %collective-permute-start = (bf16[1024,128]{1,0:T(8,128)(2,1)S(1)}, bf16[1024,128]{1,0:T(8,128)(2,1)S(1)}, u32[]{:S(2)}, u32[]{:S(2)}) collective-permute-start(bf16[1024,128]{1,0:T(8,128)(2,1)S(1)} %copy-done.23), channel_id=1, source_target_pairs={{0,4},{4,8},{8,12},{12,16},{16,20},{20,24},{24,28},{28,0},{1,5},{5... | collective-permute-start | bytes 786440 | tf_op jit(solution)/shard_map/ppermute | solution.py:22
  152.9 14.5 %collective-permute-start.1 = (bf16[1024,128]{1,0:T(8,128)(2,1)S(1)}, bf16[1024,128]{1,0:T(8,128)(2,1)S(1)}, u32[]{:S(2)}, u32[]{:S(2)}) collective-permute-start(bf16[1024,128]{1,0:T(8,128)(2,1)S(1)} %collective-permute-done), channel_id=1, source_target_pairs={{0,4},{4,8},{8,12},{12,16},{16,20},{20,24},{24,28},{28,0},{1,5},{5... | collective-permute-start | bytes 786440 | tf_op jit(solution)/shard_map/ppermute | solution.py:22
  167.3 9.1 %collective-permute-start.2 = (bf16[1024,128]{1,0:T(8,128)(2,1)S(1)}, bf16[1024,128]{1,0:T(8,128)(2,1)S(1)}, u32[]{:S(2)}, u32[]{:S(2)}) collective-permute-start(bf16[1024,128]{1,0:T(8,128)(2,1)S(1)} %collective-permute-done.1), channel_id=1, source_target_pairs={{0,4},{4,8},{8,12},{12,16},{16,20},{20,24},{24,28},{28,0},{1,5},{5... | collective-permute-start | bytes 786440 | tf_op jit(solution)/shard_map/ppermute | solution.py:22
  171.5 90.3 %reduce-scatter.13.cloned.1.call-start = ((), (), s32[]{:S(2)}) async-start(), calls=%async_computation.14 | async-start | bytes 1310720 | tf_op jit(solution)/shard_map/reduce_scatter | solution.py:155
  176.4 16.7 %collective-permute-start.3 = (bf16[1024,128]{1,0:T(8,128)(2,1)S(1)}, bf16[1024,128]{1,0:T(8,128)(2,1)S(1)}, u32[]{:S(2)}, u32[]{:S(2)}) collective-permute-start(bf16[1024,128]{1,0:T(8,128)(2,1)S(1)} %collective-permute-done.2), channel_id=1, source_target_pairs={{0,4},{4,8},{8,12},{12,16},{16,20},{20,24},{24,28},{28,0},{1,5},{5... | collective-permute-start | bytes 786440 | tf_op jit(solution)/shard_map/ppermute | solution.py:22
  193.1 15.6 %collective-permute-start.4 = (bf16[1024,128]{1,0:T(8,128)(2,1)S(1)}, bf16[1024,128]{1,0:T(8,128)(2,1)}, u32[]{:S(2)}, u32[]{:S(2)}) collective-permute-start(bf16[1024,128]{1,0:T(8,128)(2,1)S(1)} %collective-permute-done.3), channel_id=1, source_target_pairs={{0,4},{4,8},{8,12},{12,16},{16,20},{20,24},{24,28},{28,0},{1,5},{5... | collective-permute-start | bytes 786440 | tf_op jit(solution)/shard_map/ppermute | solution.py:22
  208.7 11.3 %collective-permute-start.5 = (bf16[1024,128]{1,0:T(8,128)(2,1)}, bf16[1024,128]{1,0:T(8,128)(2,1)S(1)}, u32[]{:S(2)}, u32[]{:S(2)}) collective-permute-start(bf16[1024,128]{1,0:T(8,128)(2,1)} %collective-permute-done.4), channel_id=1, source_target_pairs={{0,4},{4,8},{8,12},{12,16},{16,20},{20,24},{24,28},{28,0},{1,5},{5... | collective-permute-start | bytes 786440 | tf_op jit(solution)/shard_map/ppermute | solution.py:22
  220.0 9.1 %collective-permute-start.6 = (bf16[1024,128]{1,0:T(8,128)(2,1)S(1)}, bf16[1024,128]{1,0:T(8,128)(2,1)S(1)}, u32[]{:S(2)}, u32[]{:S(2)}) collective-permute-start(bf16[1024,128]{1,0:T(8,128)(2,1)S(1)} %collective-permute-done.5), channel_id=1, source_target_pairs={{0,4},{4,8},{8,12},{12,16},{16,20},{20,24},{24,28},{28,0},{1,5},{5... | collective-permute-start | bytes 786440 | tf_op jit(solution)/shard_map/ppermute | solution.py:22
  239.4 42.0 %all-gather.12.cloned.1.call-start = ((), (), s32[]{:S(2)}) async-start(), calls=%async_computation.15 | async-start | bytes 1310720 | tf_op jit(solution)/shard_map/all_gather | solution.py:167
  264.7 49.5 %reduce-scatter.15.cloned.1.call-start = ((), (), s32[]{:S(2)}) async-start(), calls=%async_computation.16 | async-start | bytes 1310720 | tf_op jit(solution)/shard_map/reduce_scatter | solution.py:173
  289.3 45.0 %all-gather.14.cloned.1.call-start = ((), (), s32[]{:S(2)}) async-start(), calls=%async_computation.17 | async-start | bytes 1310720 | tf_op jit(solution)/shard_map/all_gather | solution.py:181
  317.6 106.7 %reduce-scatter.23.cloned.1.call-start = ((), (), s32[]{:S(2)}) async-start(), calls=%async_computation.21 | async-start | bytes 1179648 | tf_op jit(solution)/shard_map/reduce_scatter | solution.py:229
  341.0 132.2 %reduce-scatter.21.cloned.1.call-start = ((), (), s32[]{:S(2)}) async-start(), calls=%async_computation.20 | async-start | bytes 1179648 | tf_op jit(solution)/shard_map/reduce_scatter | solution.py:228
  353.7 186.5 %reduce-scatter.19.cloned.1.call-start = ((), (), s32[]{:S(2)}) async-start(), calls=%async_computation.19 | async-start | bytes 1179648 | tf_op jit(solution)/shard_map/reduce_scatter | solution.py:227
  365.3 201.0 %reduce-scatter.17.cloned.1.call-start = ((), (), s32[]{:S(2)}) async-start(), calls=%async_computation.18 | async-start | bytes 1310720 | tf_op jit(solution)/shard_map/reduce_scatter | solution.py:215
  370.1 264.9 %reduce-scatter.25.cloned.1.call-start = ((), (), s32[]{:S(2)}) async-start(), calls=%async_computation.22 | async-start | bytes 1179648 | tf_op jit(solution)/shard_map/reduce_scatter | solution.py:233
  371.6 355.3 %reduce-scatter.29.cloned.1.call-start = ((), (), s32[]{:S(2)}) async-start(), calls=%async_computation.24 | async-start | bytes 4718592 | tf_op jit(solution)/shard_map/reduce_scatter | solution.py:234
  376.2 442.5 %reduce-scatter.27.cloned.1.call-start = ((), (), s32[]{:S(2)}) async-start(), calls=%async_computation.23 | async-start | bytes 4718592 | tf_op jit(solution)/shard_map/reduce_scatter | solution.py:230
  (32 other events, 420.1 us)
Sparse Core Ops, SparseCore 0:
  10.4 19.4 all-gather.5
  143.2 24.0 reduce-scatter.10
  239.5 22.2 reduce-scatter.12
  289.4 24.7 reduce-scatter.14
Sparse Core Ops, SparseCore 1:
  145.7 58.0 all-gather.9
  205.8 19.6 all-gather.7
  264.8 16.5 all-gather.11
  317.7 16.5 all-gather.13
  341.1 64.8 reduce-scatter.22
  409.4 63.7 reduce-scatter.20
  476.4 63.7 reduce-scatter.18
  542.6 23.7 reduce-scatter.16
  570.2 64.7 reduce-scatter.24
  639.2 87.6 reduce-scatter.28
  730.9 87.8 reduce-scatter.26
